TPU v7x, 32 devices: a whole 2x2x4 slice. The times are simulated.
32 devices in a mesh: dp: 4 (over y, x), token: 8 (over z, core).
Axes of the slice: x: 2, y: 2, z: 4, core: 2. Of those that a mesh axis runs over, the one named last changes fastest.
Arguments:
- mix_input: bfloat16 [1536, 8, 768], P('dp', 'token'), may hold values from -6 to 6
- out_grad: bfloat16 [1536, 8, 768], P('dp', 'token'), may hold values from -1.5 to 1.5
- w_up: bfloat16 [8, 768, 3072], P('token'), may hold values from -0.21875 to 0.21875
- w_down: bfloat16 [8, 3072, 768], P('token'), may hold values from -0.109375 to 0.109375
- gain_first: float32 [8, 768], P('token'), may hold values from 0.25 to 1.75
- gain_second: float32 [8, 768], P('token'), may hold values from 0.25 to 1.75
- owner_dev: int32 [8, 1536, 1], P('token', 'dp'), may hold values from 0 to 3; in each aligned block of 384 rows (0 to 383, 384 to 767, ..., all dimensions but the last counted through in order) at most 240 rows name the same one
- slot_row: int32 [8, 1536], P('token', 'dp'), may hold values from 0 to 255
Outputs:
- grad_up: float32 [8, 768, 3072], P('token', 'dp')
- grad_down: float32 [8, 3072, 768], P('token', 'dp')
- row_grad: float32 [8, 1024, 768], P('token', 'dp')
Inputs may be any that keep to these rules, and one draw needn't show every extreme that they name: `owner_dev`: in the rows of one device (aligned blocks of 384 samples of one token) no owner is named by more than 240 rows, a bound that some block reaches.
All inputs are finite; a program needn't handle non-finite values.
Results may differ from a plain program's by a relative error of at most 0.015.
Values may be sent and summed in bfloat16 or wider, within the bound.
A program may use at most 128 MiB of HBM per device.

v0:
```python
import functools

import jax
import jax.numpy as jnp
from jax import lax
from jax.experimental import pallas as pl
from jax.experimental.pallas import tpu as pltpu

from jax.sharding import PartitionSpec as P

HOT = 256


EPS = 1e-05
HALF_ROOT = 0.7071067811865476
INV_ROOT_TAU = 0.3989422804014327


def normalize(values):
    center = values - jnp.mean(values, axis=-1, keepdims=True)
    inv_scale = lax.rsqrt(jnp.mean(center * center, axis=-1, keepdims=True) + EPS)
    return (center * inv_scale, inv_scale)


def norm_back(grad_norm, normed, inv_scale):
    mean_grad = jnp.mean(grad_norm, axis=-1, keepdims=True)
    mean_proj = jnp.mean(grad_norm * normed, axis=-1, keepdims=True)
    return inv_scale * (grad_norm - mean_grad - normed * mean_proj)


def gelu_parts(pre_act):
    cumul = 0.5 * (1.0 + jax.scipy.special.erf(pre_act * HALF_ROOT))
    density = jnp.exp(-0.5 * pre_act * pre_act) * INV_ROOT_TAU
    return (pre_act * cumul, cumul + pre_act * density)


def contract_rows(left, right):
    return lax.dot_general(
        left, right, (((0,), (0,)), ((), ())), preferred_element_type=jnp.float32
    )


def contract_cols(left, right):
    return lax.dot_general(
        left, right, (((1,), (1,)), ((), ())), preferred_element_type=jnp.float32
    )


def per_device(mix_input, out_grad, w_up, w_down, gain_first, gain_second, owner_dev, slot_row):
    batch_rows = mix_input.shape[0]
    width = mix_input.shape[2]
    owners = lax.axis_size("dp")
    normed, inv_scale = normalize(mix_input[:, 0, :].astype(jnp.float32))
    hidden_in = (normed * gain_first[0]).astype(jnp.bfloat16)
    pre_act = jnp.dot(hidden_in, w_up[0], preferred_element_type=jnp.float32)
    act_value, act_slope = gelu_parts(pre_act)
    active = act_value.astype(jnp.bfloat16)
    outer_sum = jnp.dot(active, w_down[0], preferred_element_type=jnp.float32) + hidden_in.astype(
        jnp.float32
    )
    normed_out, inv_out = normalize(outer_sum)
    grad_wide = norm_back(
        out_grad[:, 0, :].astype(jnp.float32) * gain_second[0], normed_out, inv_out
    )
    grad_mid = grad_wide.astype(jnp.bfloat16)
    grad_act = contract_cols(grad_mid, w_down[0])
    grad_pre = (grad_act * act_slope).astype(jnp.bfloat16)
    up_whole = contract_rows(hidden_in, grad_pre)
    down_whole = contract_rows(active, grad_mid)
    grad_up, grad_down = (
        lax.psum_scatter(
            up_whole.astype(jnp.bfloat16), "dp", scatter_dimension=0, tiled=True
        ).astype(jnp.float32),
        lax.psum_scatter(
            down_whole.astype(jnp.bfloat16), "dp", scatter_dimension=0, tiled=True
        ).astype(jnp.float32),
    )
    grad_hidden = contract_cols(grad_pre, w_up[0]) + grad_wide
    grad_sum = norm_back(grad_hidden * gain_first[0], normed, inv_scale).astype(jnp.bfloat16)
    pieces = lax.axis_size("token")
    swapped = lax.all_to_all(
        grad_sum.reshape(batch_rows, pieces, width // pieces),
        "token",
        split_axis=1,
        concat_axis=1,
        tiled=True,
    )
    embed_grad = (
        grad_sum.astype(jnp.float32) + swapped.reshape(batch_rows, width).astype(jnp.float32)
    ).astype(jnp.bfloat16)
    owner_ids = owner_dev[0, :, 0]
    slot_ids = slot_row[0]
    capacity = max(2, 8 * (5 * batch_rows // (16 * owners)))
    owner_hot = (
        owner_ids[:, None] == lax.broadcasted_iota(jnp.int32, (batch_rows, owners), 1)
    ).astype(jnp.int32)
    rank_within = jnp.sum((jnp.cumsum(owner_hot, axis=0) - 1) * owner_hot, axis=1)
    place = owner_ids * capacity + rank_within
    dispatch_mask = (
        lax.broadcasted_iota(jnp.int32, (owners * capacity, batch_rows), 0) == place[None, :]
    )
    send_grad = jnp.dot(
        dispatch_mask.astype(jnp.bfloat16), embed_grad, preferred_element_type=jnp.float32
    )
    send_grad = send_grad.astype(jnp.bfloat16).reshape(owners, capacity, width)
    send_slot = jnp.sum(dispatch_mask.astype(jnp.int32) * (slot_ids + 1)[None, :], axis=1) - 1
    send_slot = send_slot.astype(jnp.float32).astype(jnp.bfloat16).reshape(owners, capacity)
    recv_grad, recv_slot = (
        lax.all_to_all(send_grad, "dp", split_axis=0, concat_axis=0, tiled=True),
        lax.all_to_all(send_slot, "dp", split_axis=0, concat_axis=0, tiled=True),
    )
    slot_values = recv_slot.reshape(1, owners * capacity).astype(jnp.float32)
    gather_hot = (
        lax.broadcasted_iota(jnp.int32, (HOT, owners * capacity), 0).astype(jnp.float32)
        == slot_values
    ).astype(jnp.bfloat16)
    row_grad = jnp.dot(
        gather_hot, recv_grad.reshape(owners * capacity, width), preferred_element_type=jnp.float32
    )
    return (grad_up[None], grad_down[None], row_grad[None])


SUB = 256
VMEM_BYTES = 67043328
MESH = pl.DeviceIdType.MESH


def contract_flat(left, right):
    return jnp.dot(left, right, preferred_element_type=jnp.float32)


def fused_kernel(
    n_tok,
    mix_in, grad_in, up_in, down_in, gain1_in, gain2_in, owner_in, slot_in,
    gup_out, gdown_out, rows_out,
    mix_v, mid_v, h_v, up_v, down_v, slope_v, act_v, hsel_v, gup_v, gdown_v, wide_v, acc_v, grad_v,
    sum_v, swap_v, embed_v, far_v, part_v, back_v, mine_v, gain1_v, gain2_v, owner_v, slot_v,
    up_sem, down_sem, load_sem, out_sem, send_sem, recv_sem, swap_send, swap_recv,
):
    rows, width = grad_v.shape
    chunks, _, part = up_v.shape
    piece = width // n_tok
    half_w = width // 2
    half_r = rows // 2
    hot_rows = rows_out.shape[0]
    bf, f32 = jnp.bfloat16, jnp.float32
    me = lax.axis_index("dp")
    tok = lax.axis_index("token")
    col = lax.rem(me, 2)
    over_x = {"dp": me + 1 - 2 * col}
    over_y = {"dp": lax.rem(me + 2, 4)}

    def group(g):
        return pl.ds(g * rows, rows)

    def chunk_at(j):
        return lax.rem(j + me + 1, chunks)

    def remote(i, src, dst, device):
        return pltpu.make_async_remote_copy(
            src_ref=src, dst_ref=dst, send_sem=send_sem.at[i], recv_sem=recv_sem.at[i],
            device_id=device, device_id_type=MESH,
        )

    def load_up(j):
        c = chunk_at(j)
        cols = pl.ds(pl.multiple_of(c * part, part), part)
        return pltpu.make_async_copy(up_in.at[:, cols], up_v.at[c], up_sem.at[j])

    def load_down(j):
        c = chunk_at(j)
        lines = pl.ds(pl.multiple_of(c * part, part), part)
        return pltpu.make_async_copy(down_in.at[lines, :], down_v.at[c], down_sem.at[j])

    small = [
        (mix_in, mix_v.at[group(0)]),
        (gain1_in, gain1_v),
        (gain2_in, gain2_v),
        (grad_in, grad_v),
        (owner_in, owner_v.at[0]),
        (slot_in, slot_v.at[0]),
    ]
    loads = [pltpu.make_async_copy(s, d, load_sem.at[i]) for i, (s, d) in enumerate(small)]
    loads[0].start()
    loads[1].start()
    for j in range(chunks):
        load_up(j).start()
        load_down(j).start()
    for load in loads[2:]:
        load.start()

    barrier = pltpu.get_barrier_semaphore()
    for device in (over_x, over_y):
        pl.semaphore_signal(barrier, inc=1, device_id=device, device_id_type=MESH)
    for k in range(1, n_tok):
        peer = {"token": lax.rem(tok + k, n_tok)}
        pl.semaphore_signal(barrier, inc=1, device_id=peer, device_id_type=MESH)
    pl.semaphore_wait(barrier, n_tok + 1)

    mix_x = remote(0, mix_in, mix_v.at[group(1)], over_x)
    mix_y = remote(1, mix_in, mix_v.at[group(2)], over_y)
    ids = [
        remote(2, owner_in, owner_v.at[1], over_x),
        remote(3, slot_in, slot_v.at[1], over_x),
        remote(4, owner_in, owner_v.at[2], over_y),
        remote(5, slot_in, slot_v.at[2], over_y),
    ]
    for copy in [mix_x, mix_y] + ids:
        copy.start()

    def norm_group(g):
        normed, _ = normalize(mix_v[group(g), :].astype(f32))
        h_v[group(g), :] = (normed * gain1_v[...]).astype(bf)

    def pick_group(g):
        shape = (hsel_v.shape[0], width)
        row = lax.broadcasted_iota(jnp.int32, shape, 0) + me * shape[0]
        pick = (row == lax.broadcasted_iota(jnp.int32, shape, 1)).astype(bf)
        hsel_v[:, group(g)] = contract_cols(pick, h_v[group(g), :]).astype(bf)

    def activate(g, c):
        pres = [
            contract_flat(h_v[group(g), :], up_v[c, :, s : s + SUB]) for s in range(0, part, SUB)
        ]
        total = None
        for i, pre in enumerate(pres):
            cols = slice(i * SUB, (i + 1) * SUB)
            value, slope = gelu_parts(pre)
            act = value.astype(bf)
            act_v[group(g), cols] = act
            slope_v[c, group(g), cols] = slope.astype(bf)
            if g == 0:
                more = contract_flat(act, down_v[c, cols, :])
                total = more if total is None else total + more
        return total

    loads[0].wait()
    loads[1].wait()
    norm_group(0)
    acc_v[...] = h_v[group(0), :].astype(f32)

    @pl.loop(0, chunks)
    def _(j):
        load_up(j).wait()
        load_down(j).wait()
        acc_v[...] += activate(0, chunk_at(j))

    for load in loads[2:]:
        load.wait()
    normed, inv = normalize(acc_v[...])
    wide = norm_back(grad_v[...].astype(f32) * gain2_v[...], normed, inv)
    wide_v[...] = wide
    mid_v[group(0), :] = wide.astype(bf)
    mid_x = remote(6, mid_v.at[group(0)], mid_v.at[group(1)], over_x)
    mid_y = remote(7, mid_v.at[group(0)], mid_v.at[group(2)], over_y)
    mid_x.start()
    mid_y.start()

    def slope_group(g, c):
        grad_act = contract_cols(mid_v[group(g), :], down_v[c])
        grad_pre = (grad_act * slope_v[c, group(g), :].astype(f32)).astype(bf)
        slope_v[c, group(g), :] = grad_pre
        return grad_pre

    acc_v[...] = wide_v[...]

    @pl.loop(0, chunks)
    def _(c):
        acc_v[...] += contract_cols(slope_group(0, c), up_v[c])

    normed, inv = normalize(mix_v[group(0), :].astype(f32))
    grad_sum = norm_back(acc_v[...] * gain1_v[...], normed, inv)
    sum_v[...] = grad_sum.T.astype(bf)

    own_piece = pl.ds(pl.multiple_of(tok * piece, piece), piece)
    swaps = []
    for k in range(1, n_tok):
        peer = lax.rem(tok + k, n_tok)
        there = pl.ds(pl.multiple_of(peer * piece, piece), piece)
        swaps.append(
            pltpu.make_async_remote_copy(
                src_ref=sum_v.at[there], dst_ref=swap_v.at[own_piece],
                send_sem=swap_send.at[k - 1], recv_sem=swap_recv.at[k - 1],
                device_id={"token": peer}, device_id_type=MESH,
            )
        )
        swaps[-1].start()
    swap_v[own_piece, :] = sum_v[own_piece, :]

    first, second = pl.ds(0, half_r), pl.ds(half_r, half_r)

    def block(ref, g, part_of):
        return ref.at[pl.ds(g * rows + part_of * half_r, half_r)]

    mix_x.wait_recv()
    mix_dx = remote(8, block(mix_v, 1, 0), block(mix_v, 3, 0), over_y)
    mix_dx.start()
    mix_y.wait_recv()
    mix_dy = remote(9, block(mix_v, 2, 1), block(mix_v, 3, 1), over_x)
    mix_dy.start()

    def others(g):
        norm_group(g)
        pick_group(g)

        @pl.loop(0, chunks)
        def _(j):
            activate(g, chunk_at(j))

    pick_group(0)
    others(1)
    others(2)

    for copy in swaps:
        copy.wait_recv()
    embed_v[...] = (sum_v[...].astype(f32) + swap_v[...].astype(f32)).astype(bf)
    low, high = pl.ds(0, half_w), pl.ds(half_w, half_w)
    far_x = remote(10, embed_v.at[low], far_v.at[0], over_x)
    far_y = remote(11, embed_v.at[high], far_v.at[1], over_y)
    far_x.start()
    far_y.start()

    mid_x.wait_recv()
    mid_dx = remote(12, block(mid_v, 1, 0), block(mid_v, 3, 0), over_y)
    mid_dx.start()
    mid_y.wait_recv()
    mid_dy = remote(13, block(mid_v, 2, 1), block(mid_v, 3, 1), over_x)
    mid_dy.start()

    pair = pl.ds(0, 2 * rows)

    @pl.loop(0, chunks)
    def _(c):
        slope_group(1, c)
        gup_v[c] = contract_flat(hsel_v[:, pair], slope_v[c, pair, :])

    gdown_v[...] = contract_rows(act_v[pair, :], mid_v[pair, :])

    @pl.loop(0, chunks)
    def _(c):
        grad_pre = slope_group(2, c)
        gup_v[c] += contract_flat(hsel_v[:, group(2)], grad_pre)

    gdown_v[...] += contract_rows(act_v[group(2), :], mid_v[group(2), :])

    mix_dx.wait_recv()
    mix_dy.wait_recv()
    others(3)

    for copy in ids:
        copy.wait_recv()
    far_x.wait_recv()
    far_y.wait_recv()

    def hot(k, owner):
        target = owner_v[k] * hot_rows + slot_v[k]
        row = lax.broadcasted_iota(jnp.int32, (hot_rows, rows), 0) + owner * hot_rows
        return (row == target).astype(bf)

    def merge(owner, k, cols):
        kept = contract_cols(hot(0, owner), embed_v[cols, :])
        return kept + contract_cols(hot(k, owner), far_v[k - 1])

    part_v[0] = merge(over_y["dp"], 1, low).astype(bf)
    part_v[1] = merge(over_x["dp"], 2, high).astype(bf)
    back_y = remote(14, part_v.at[0], back_v.at[0], over_y)
    back_x = remote(15, part_v.at[1], back_v.at[1], over_x)
    back_y.start()
    back_x.start()
    mine_v[:, :half_w] = merge(me, 1, low)
    mine_v[:, half_w:] = merge(me, 2, high)

    mid_dx.wait_recv()
    mid_dy.wait_recv()

    def store_up(c):
        cols = pl.ds(pl.multiple_of(c * part, part), part)
        return pltpu.make_async_copy(gup_v.at[c], gup_out.at[:, cols], up_sem.at[c])

    @pl.loop(0, chunks)
    def _(c):
        grad_pre = slope_group(3, c)
        gup_v[c] += contract_flat(hsel_v[:, group(3)], grad_pre)
        store_up(c).start()

    gdown_v[...] += contract_rows(act_v[group(3), :], mid_v[group(3), :])
    store_down = pltpu.make_async_copy(gdown_v, gdown_out, out_sem.at[0])
    store_down.start()

    back_y.wait_recv()
    back_x.wait_recv()
    mine_v[:, :half_w] += back_v[0].astype(f32)
    mine_v[:, half_w:] += back_v[1].astype(f32)
    store_rows = pltpu.make_async_copy(mine_v, rows_out, out_sem.at[1])
    store_rows.start()

    for copy in [mix_x, mix_y] + ids + [mid_x, mid_y, mix_dx, mix_dy] + swaps:
        copy.wait_send()
    for copy in [far_x, far_y, mid_dx, mid_dy, back_x, back_y]:
        copy.wait_send()
    for c in range(chunks):
        store_up(c).wait()
    store_down.wait()
    store_rows.wait()


def small_group(mix_input, out_grad, w_up, w_down, gain_first, gain_second, owner_dev, slot_row):
    rows = mix_input.shape[0]
    width = mix_input.shape[2]
    hidden = w_up.shape[2]
    groups = lax.axis_size("dp")
    n_tok = lax.axis_size("token")
    part = hidden // groups
    own = width // groups
    half = width // 2
    bf, f32, i32 = jnp.bfloat16, jnp.float32, jnp.int32
    vm, dma = pltpu.VMEM, pltpu.SemaphoreType.DMA
    anywhere = pl.BlockSpec(memory_space=pl.ANY)
    unit = 2 * rows * width * hidden
    grad_up, grad_down, row_grad = pl.pallas_call(
        functools.partial(fused_kernel, n_tok),
        in_specs=[anywhere] * 8,
        out_specs=[anywhere] * 3,
        out_shape=[
            jax.ShapeDtypeStruct((own, hidden), f32),
            jax.ShapeDtypeStruct((part, width), f32),
            jax.ShapeDtypeStruct((HOT, width), f32),
        ],
        scratch_shapes=[
            vm((groups * rows, width), bf),
            vm((groups * rows, width), bf),
            vm((groups * rows, width), bf),
            vm((groups, width, part), bf),
            vm((groups, part, width), bf),
            vm((groups, groups * rows, part), bf),
            vm((groups * rows, part), bf),
            vm((own, groups * rows), bf),
            vm((groups, own, part), f32),
            vm((part, width), f32),
            vm((rows, width), f32),
            vm((rows, width), f32),
            vm((rows, width), bf),
            vm((width, rows), bf),
            vm((width, rows), bf),
            vm((width, rows), bf),
            vm((2, half, rows), bf),
            vm((2, HOT, half), bf),
            vm((2, HOT, half), bf),
            vm((HOT, width), f32),
            vm((1, width), f32),
            vm((1, width), f32),
            vm((3, 1, rows), i32),
            vm((3, 1, rows), i32),
            dma((groups,)),
            dma((groups,)),
            dma((6,)),
            dma((2,)),
            dma((16,)),
            dma((16,)),
            dma((n_tok - 1,)),
            dma((n_tok - 1,)),
        ],
        compiler_params=pltpu.CompilerParams(
            vmem_limit_bytes=VMEM_BYTES, collective_id=0, has_side_effects=True
        ),
        cost_estimate=pl.CostEstimate(
            flops=12 * unit, bytes_accessed=8 * width * hidden, transcendentals=0
        ),
        name="fused",
    )(
        mix_input[:, 0, :], out_grad[:, 0, :], w_up[0], w_down[0], gain_first, gain_second,
        owner_dev[:, :, 0], slot_row,
    )
    return (grad_up[None], grad_down[None], row_grad[None])


def solution(mesh):
    placed = (
        P("dp", "token", None),
        P("dp", "token", None),
        P("token", None, None),
        P("token", None, None),
        P("token", None),
        P("token", None),
        P("token", "dp", None),
        P("token", "dp"),
    )
    small = mesh.shape["dp"] == 4
    return jax.shard_map(
        small_group if small else per_device,
        mesh=mesh,
        in_specs=placed,
        out_specs=(P("token", "dp", None), P("token", "dp", None), P("token", "dp", None)),
        check_vma=False,
    )
```

profile of v0, /device:TPU:0, one launch (start us, length us, event | category | flops | bytes accessed | tf_op | source)
XLA Modules:
  0.0 66.5 jit_solution(12448898867287303493)
XLA Ops:
  0.6 59.8 %fused.1 = (f32[192,3072]{1,0:T(8,128)}, f32[768,768]{1,0:T(8,128)}, f32[256,768]{1,0:T(8,128)}) custom-call(bf16[384,768]{1,0:T(8,128)(2,1)} %bitcast.13, bf16[384,768]{1,0:T(8,128)(2,1)} %bitcast.14, bf16[768,3072]{1,0:T(8,128)(2,1)} %bitcast.11, bf16[3072,768]{1,0:T(8,128)(2,1)} %bitcast.12, f32[1,768]{1,0:T(1,128)} %gain1_in.1, f32[1,768]{1,0:T(1,128)} %gain2_in.1, ...), custom_call_target="tpu_custom_call" | custom-call | flops 21743271936 | bytes 18874368 | tf_op jit(solution)/shard_map/fused/pallas_call | solution.py:420
  60.4 0.0 copy-start
  60.5 3.4 %copy.14 = f32[1,192,3072]{2,1,0:T(8,128)} copy(f32[1,192,3072]{2,1,0:T(8,128)} %bitcast.9) | data formatting | bytes 4718592
  63.9 0.0 copy-done
  63.9 0.0 copy-start.1
  63.9 1.4 %copy.15 = f32[1,768,768]{2,1,0:T(8,128)} copy(f32[1,768,768]{2,1,0:T(8,128)S(1)} %bitcast.8) | data formatting | bytes 4718592
  65.3 0.3 copy-done.1
  65.6 0.9 %copy.16 = f32[1,256,768]{2,1,0:T(8,128)} copy(f32[1,256,768]{2,1,0:T(8,128)S(1)} %bitcast.10) | data formatting | bytes 1572864
Async XLA Ops:
  60.4 3.5 %copy-start = (f32[768,768]{1,0:T(8,128)S(1)}, f32[768,768]{1,0:T(8,128)}, u32[]{:S(2)}) copy-start(f32[768,768]{1,0:T(8,128)} %get-tuple-element.7) | copy-start | bytes 7077892
  63.9 1.7 %copy-start.1 = (f32[256,768]{1,0:T(8,128)S(1)}, f32[256,768]{1,0:T(8,128)}, u32[]{:S(2)}) copy-start(f32[256,768]{1,0:T(8,128)} %get-tuple-element.8) | copy-start | bytes 2359300
where the time goes:
time: 66.6 us; the launch traced here: 66.5 us
  Pallas kernels  59.8 us (90%)
  local copies, waits for them, and re-layouts  6.01 us (9%)
    pallas_call x1, Pallas kernels, small_group(): pl.pallas_call(functools.partial(fused_kernel, n_tok), in_specs=[anywhere...  59.8 us
    unnamed x7, local copies, waits for them, and re-layouts  6.01 us

commit v1 on v0

--- a/solution.py
+++ b/solution.py
@@ -121,7 +121,7 @@
 
 
 SUB = 256
-VMEM_BYTES = 67043328
+VMEM_BYTES = 56 * 1024 * 1024
 MESH = pl.DeviceIdType.MESH
 
 
@@ -132,17 +132,17 @@
 def fused_kernel(
     n_tok,
     mix_in, grad_in, up_in, down_in, gain1_in, gain2_in, owner_in, slot_in,
-    gup_out, gdown_out, rows_out,
-    mix_v, mid_v, h_v, up_v, down_v, slope_v, act_v, hsel_v, gup_v, gdown_v, wide_v, acc_v, grad_v,
-    sum_v, swap_v, embed_v, far_v, part_v, back_v, mine_v, gain1_v, gain2_v, owner_v, slot_v,
-    up_sem, down_sem, load_sem, out_sem, send_sem, recv_sem, swap_send, swap_recv,
+    gup_v, gdown_v, mine_v,
+    mix_v, mid_v, h_v, up_v, down_v, slope_v, act_v, hsel_v, wide_v, acc_v, grad_v,
+    sum_v, swap_v, embed_v, far_v, part_v, back_v, gain1_v, gain2_v, owner_v, slot_v,
+    up_sem, down_sem, load_sem, send_sem, recv_sem, swap_send, swap_recv,
 ):
     rows, width = grad_v.shape
     chunks, _, part = up_v.shape
     piece = width // n_tok
     half_w = width // 2
     half_r = rows // 2
-    hot_rows = rows_out.shape[0]
+    hot_rows = mine_v.shape[0]
     bf, f32 = jnp.bfloat16, jnp.float32
     me = lax.axis_index("dp")
     tok = lax.axis_index("token")
@@ -197,8 +197,9 @@
         pl.semaphore_signal(barrier, inc=1, device_id=peer, device_id_type=MESH)
     pl.semaphore_wait(barrier, n_tok + 1)
 
-    mix_x = remote(0, mix_in, mix_v.at[group(1)], over_x)
-    mix_y = remote(1, mix_in, mix_v.at[group(2)], over_y)
+    loads[0].wait()
+    mix_x = remote(0, mix_v.at[group(0)], mix_v.at[group(1)], over_x)
+    mix_y = remote(1, mix_v.at[group(0)], mix_v.at[group(2)], over_y)
     ids = [
         remote(2, owner_in, owner_v.at[1], over_x),
         remote(3, slot_in, slot_v.at[1], over_x),
@@ -234,7 +235,6 @@
                 total = more if total is None else total + more
         return total
 
-    loads[0].wait()
     loads[1].wait()
     norm_group(0)
     acc_v[...] = h_v[group(0), :].astype(f32)
@@ -373,35 +373,41 @@
     mid_dx.wait_recv()
     mid_dy.wait_recv()
 
-    def store_up(c):
-        cols = pl.ds(pl.multiple_of(c * part, part), part)
-        return pltpu.make_async_copy(gup_v.at[c], gup_out.at[:, cols], up_sem.at[c])
-
     @pl.loop(0, chunks)
     def _(c):
         grad_pre = slope_group(3, c)
         gup_v[c] += contract_flat(hsel_v[:, group(3)], grad_pre)
-        store_up(c).start()
 
     gdown_v[...] += contract_rows(act_v[group(3), :], mid_v[group(3), :])
-    store_down = pltpu.make_async_copy(gdown_v, gdown_out, out_sem.at[0])
-    store_down.start()
 
     back_y.wait_recv()
     back_x.wait_recv()
     mine_v[:, :half_w] += back_v[0].astype(f32)
     mine_v[:, half_w:] += back_v[1].astype(f32)
-    store_rows = pltpu.make_async_copy(mine_v, rows_out, out_sem.at[1])
-    store_rows.start()
 
     for copy in [mix_x, mix_y] + ids + [mid_x, mid_y, mix_dx, mix_dy] + swaps:
         copy.wait_send()
     for copy in [far_x, far_y, mid_dx, mid_dy, back_x, back_y]:
         copy.wait_send()
+
+
+def store_kernel(up_ref, down_ref, rows_ref, up_out, down_out, rows_out, sems):
+    chunks, _, part = up_ref.shape
+    copies = [
+        pltpu.make_async_copy(up_ref.at[c], up_out.at[:, pl.ds(c * part, part)], sems.at[c])
+        for c in range(chunks)
+    ]
+    quarter = part // chunks
     for c in range(chunks):
-        store_up(c).wait()
-    store_down.wait()
-    store_rows.wait()
+        lines = pl.ds(c * quarter, quarter)
+        copies.append(
+            pltpu.make_async_copy(down_ref.at[lines], down_out.at[lines], sems.at[chunks + c])
+        )
+    copies.append(pltpu.make_async_copy(rows_ref, rows_out, sems.at[2 * chunks]))
+    for copy in copies:
+        copy.start()
+    for copy in copies:
+        copy.wait()
 
 
 def small_group(mix_input, out_grad, w_up, w_down, gain_first, gain_second, owner_dev, slot_row):
@@ -415,17 +421,14 @@
     half = width // 2
     bf, f32, i32 = jnp.bfloat16, jnp.float32, jnp.int32
     vm, dma = pltpu.VMEM, pltpu.SemaphoreType.DMA
-    anywhere = pl.BlockSpec(memory_space=pl.ANY)
+    main = pl.BlockSpec(memory_space=pltpu.HBM)
+    inside = pl.BlockSpec(memory_space=pltpu.VMEM)
     unit = 2 * rows * width * hidden
-    grad_up, grad_down, row_grad = pl.pallas_call(
+    held = pl.pallas_call(
         functools.partial(fused_kernel, n_tok),
-        in_specs=[anywhere] * 8,
-        out_specs=[anywhere] * 3,
-        out_shape=[
-            jax.ShapeDtypeStruct((own, hidden), f32),
-            jax.ShapeDtypeStruct((part, width), f32),
-            jax.ShapeDtypeStruct((HOT, width), f32),
-        ],
+        in_specs=[main] * 8,
+        out_specs=[inside] * 3,
+        out_shape=[vm((groups, own, part), f32), vm((part, width), f32), vm((HOT, width), f32)],
         scratch_shapes=[
             vm((groups * rows, width), bf),
             vm((groups * rows, width), bf),
@@ -435,8 +438,6 @@
             vm((groups, groups * rows, part), bf),
             vm((groups * rows, part), bf),
             vm((own, groups * rows), bf),
-            vm((groups, own, part), f32),
-            vm((part, width), f32),
             vm((rows, width), f32),
             vm((rows, width), f32),
             vm((rows, width), bf),
@@ -446,7 +447,6 @@
             vm((2, half, rows), bf),
             vm((2, HOT, half), bf),
             vm((2, HOT, half), bf),
-            vm((HOT, width), f32),
             vm((1, width), f32),
             vm((1, width), f32),
             vm((3, 1, rows), i32),
@@ -454,7 +454,6 @@
             dma((groups,)),
             dma((groups,)),
             dma((6,)),
-            dma((2,)),
             dma((16,)),
             dma((16,)),
             dma((n_tok - 1,)),
@@ -471,6 +470,19 @@
         mix_input[:, 0, :], out_grad[:, 0, :], w_up[0], w_down[0], gain_first, gain_second,
         owner_dev[:, :, 0], slot_row,
     )
+    grad_up, grad_down, row_grad = pl.pallas_call(
+        store_kernel,
+        in_specs=[pl.BlockSpec(memory_space=pl.ANY)] * 3,
+        out_specs=[main] * 3,
+        out_shape=[
+            jax.ShapeDtypeStruct((own, hidden), f32),
+            jax.ShapeDtypeStruct((part, width), f32),
+            jax.ShapeDtypeStruct((HOT, width), f32),
+        ],
+        scratch_shapes=[dma((2 * groups + 1,))],
+        compiler_params=pltpu.CompilerParams(vmem_limit_bytes=1 << 20),
+        name="store",
+    )(*held)
     return (grad_up[None], grad_down[None], row_grad[None])
 
 

time: 66.6 us -> 61.4 us (0.922)
  local copies, waits for them, and re-layouts: 6.01 us -> 0 us
  Pallas kernels: 59.8 us -> 60.5 us
    unnamed x7 -> x0, local copies, waits for them, and re-layouts: 6.01 us -> none
    pallas_call x1 -> x2, Pallas kernels: 59.8 us -> 60.5 us  [the longest x1 58 us: small_group(): pl.pallas_call(functools.partial(fused_kernel, n_tok), in_specs=[main] *...]
where the time goes in v1:
time: 61.4 us; the launch traced here: 61.3 us
  Pallas kernels  60.5 us (99%)
  between operations  0.8 us (1%)
    pallas_call x1, Pallas kernels, small_group(): pl.pallas_call(functools.partial(fused_kernel, n_tok), in_specs=[main] *...  58 us
    pallas_call x1, Pallas kernels, small_group(): pl.pallas_call(store_kernel, in_specs=[pl.BlockSpec(memory_space=pl.ANY)]...  2.51 us

profile of v1, /device:TPU:0, one launch (start us, length us, event | category | flops | bytes accessed | tf_op | source)
XLA Modules:
  0.0 61.3 jit_solution(5051459905547858428)
XLA Ops:
  0.6 58.0 %fused.1 = (f32[4,192,768]{2,1,0:T(8,128)S(1)}, f32[768,768]{1,0:T(8,128)S(1)}, f32[256,768]{1,0:T(8,128)S(1)}) custom-call(bf16[384,768]{1,0:T(8,128)(2,1)} %bitcast.13, bf16[384,768]{1,0:T(8,128)(2,1)} %bitcast.14, bf16[768,3072]{1,0:T(8,128)(2,1)} %bitcast.8, bf16[3072,768]{1,0:T(8,128)(2,1)} %bitcast.9, f32[1,768]{1,0:T(1,128)} %gain1_in.1, ...), custom_call_target="tpu_custom_call" | custom-call | flops 21743271936 | bytes 18874368 | tf_op jit(solution)/shard_map/fused/pallas_call | solution.py:427
  58.6 2.5 %store.1 = (f32[192,3072]{1,0:T(8,128)}, f32[768,768]{1,0:T(8,128)}, f32[256,768]{1,0:T(8,128)}) custom-call(f32[4,192,768]{2,1,0:T(8,128)S(1)} %get-tuple-element.9.up_ref, f32[768,768]{1,0:T(8,128)S(1)} %get-tuple-element.10.down_ref, f32[256,768]{1,0:T(8,128)S(1)} %get-tuple-element.11.rows_ref), custom_call_target="tpu_custom_call" | custom-call | tf_op jit(solution)/shard_map/store/pallas_call | solution.py:473

commit v2 on v1

--- a/solution.py
+++ b/solution.py
@@ -121,6 +121,7 @@
 
 
 SUB = 256
+UNROLL = 4
 VMEM_BYTES = 56 * 1024 * 1024
 MESH = pl.DeviceIdType.MESH
 
@@ -135,7 +136,7 @@
     gup_v, gdown_v, mine_v,
     mix_v, mid_v, h_v, up_v, down_v, slope_v, act_v, hsel_v, wide_v, acc_v, grad_v,
     sum_v, swap_v, embed_v, far_v, part_v, back_v, gain1_v, gain2_v, owner_v, slot_v,
-    up_sem, down_sem, load_sem, send_sem, recv_sem, swap_send, swap_recv,
+    up_sem, down_sem, load_sem, send_sem, recv_sem, swap_send, swap_recv, ready_sem, go_sem,
 ):
     rows, width = grad_v.shape
     chunks, _, part = up_v.shape
@@ -192,10 +193,17 @@
     barrier = pltpu.get_barrier_semaphore()
     for device in (over_x, over_y):
         pl.semaphore_signal(barrier, inc=1, device_id=device, device_id_type=MESH)
-    for k in range(1, n_tok):
-        peer = {"token": lax.rem(tok + k, n_tok)}
-        pl.semaphore_signal(barrier, inc=1, device_id=peer, device_id_type=MESH)
-    pl.semaphore_wait(barrier, n_tok + 1)
+
+    @pl.when(tok == 0)
+    def _():
+        for k in range(1, n_tok):
+            pl.semaphore_signal(barrier, inc=1, device_id={"token": k}, device_id_type=MESH)
+        pl.semaphore_wait(barrier, 2)
+
+    @pl.when(tok != 0)
+    def _():
+        pl.semaphore_wait(barrier, 3)
+        pl.semaphore_signal(ready_sem, inc=1, device_id={"token": 0}, device_id_type=MESH)
 
     loads[0].wait()
     mix_x = remote(0, mix_v.at[group(0)], mix_v.at[group(1)], over_x)
@@ -239,7 +247,7 @@
     norm_group(0)
     acc_v[...] = h_v[group(0), :].astype(f32)
 
-    @pl.loop(0, chunks)
+    @pl.loop(0, chunks, unroll=UNROLL)
     def _(j):
         load_up(j).wait()
         load_down(j).wait()
@@ -256,6 +264,12 @@
     mid_x.start()
     mid_y.start()
 
+    @pl.when(tok == 0)
+    def _():
+        pl.semaphore_wait(ready_sem, n_tok - 1)
+        for k in range(1, n_tok):
+            pl.semaphore_signal(go_sem, inc=1, device_id={"token": k}, device_id_type=MESH)
+
     def slope_group(g, c):
         grad_act = contract_cols(mid_v[group(g), :], down_v[c])
         grad_pre = (grad_act * slope_v[c, group(g), :].astype(f32)).astype(bf)
@@ -264,13 +278,17 @@
 
     acc_v[...] = wide_v[...]
 
-    @pl.loop(0, chunks)
+    @pl.loop(0, chunks, unroll=UNROLL)
     def _(c):
         acc_v[...] += contract_cols(slope_group(0, c), up_v[c])
 
     normed, inv = normalize(mix_v[group(0), :].astype(f32))
     grad_sum = norm_back(acc_v[...] * gain1_v[...], normed, inv)
     sum_v[...] = grad_sum.T.astype(bf)
+
+    @pl.when(tok != 0)
+    def _():
+        pl.semaphore_wait(go_sem, 1)
 
     own_piece = pl.ds(pl.multiple_of(tok * piece, piece), piece)
     swaps = []
@@ -303,13 +321,34 @@
         norm_group(g)
         pick_group(g)
 
-        @pl.loop(0, chunks)
+        @pl.loop(0, chunks, unroll=UNROLL)
         def _(j):
             activate(g, chunk_at(j))
 
     pick_group(0)
     others(1)
     others(2)
+
+    def piece_of(g, k):
+        return mid_v.at[pl.ds(g * rows + k * (half_r // 2), half_r // 2)]
+
+    mid_x.wait_recv()
+    mid_y.wait_recv()
+    mid_d = [
+        remote(12, piece_of(1, 0), piece_of(3, 0), over_y),
+        remote(13, piece_of(2, 2), piece_of(3, 2), over_x),
+        remote(16, piece_of(1, 1), piece_of(3, 1), over_y),
+        remote(17, piece_of(2, 3), piece_of(3, 3), over_x),
+    ]
+    mid_d[0].start()
+    mid_d[1].start()
+
+    pair = pl.ds(0, 2 * rows)
+
+    @pl.loop(0, chunks, unroll=UNROLL)
+    def _(c):
+        slope_group(1, c)
+        gup_v[c] = contract_flat(hsel_v[:, pair], slope_v[c, pair, :])
 
     for copy in swaps:
         copy.wait_recv()
@@ -319,24 +358,12 @@
     far_y = remote(11, embed_v.at[high], far_v.at[1], over_y)
     far_x.start()
     far_y.start()
-
-    mid_x.wait_recv()
-    mid_dx = remote(12, block(mid_v, 1, 0), block(mid_v, 3, 0), over_y)
-    mid_dx.start()
-    mid_y.wait_recv()
-    mid_dy = remote(13, block(mid_v, 2, 1), block(mid_v, 3, 1), over_x)
-    mid_dy.start()
-
-    pair = pl.ds(0, 2 * rows)
-
-    @pl.loop(0, chunks)
-    def _(c):
-        slope_group(1, c)
-        gup_v[c] = contract_flat(hsel_v[:, pair], slope_v[c, pair, :])
+    mid_d[2].start()
+    mid_d[3].start()
 
     gdown_v[...] = contract_rows(act_v[pair, :], mid_v[pair, :])
 
-    @pl.loop(0, chunks)
+    @pl.loop(0, chunks, unroll=UNROLL)
     def _(c):
         grad_pre = slope_group(2, c)
         gup_v[c] += contract_flat(hsel_v[:, group(2)], grad_pre)
@@ -370,10 +397,10 @@
     mine_v[:, :half_w] = merge(me, 1, low)
     mine_v[:, half_w:] = merge(me, 2, high)
 
-    mid_dx.wait_recv()
-    mid_dy.wait_recv()
-
-    @pl.loop(0, chunks)
+    for copy in mid_d:
+        copy.wait_recv()
+
+    @pl.loop(0, chunks, unroll=UNROLL)
     def _(c):
         grad_pre = slope_group(3, c)
         gup_v[c] += contract_flat(hsel_v[:, group(3)], grad_pre)
@@ -387,7 +414,7 @@
 
     for copy in [mix_x, mix_y] + ids + [mid_x, mid_y, mix_dx, mix_dy] + swaps:
         copy.wait_send()
-    for copy in [far_x, far_y, mid_dx, mid_dy, back_x, back_y]:
+    for copy in [far_x, far_y, back_x, back_y] + mid_d:
         copy.wait_send()
 
 
@@ -454,10 +481,12 @@
             dma((groups,)),
             dma((groups,)),
             dma((6,)),
-            dma((16,)),
-            dma((16,)),
+            dma((18,)),
+            dma((18,)),
             dma((n_tok - 1,)),
             dma((n_tok - 1,)),
+            pltpu.SemaphoreType.REGULAR,
+            pltpu.SemaphoreType.REGULAR,
         ],
         compiler_params=pltpu.CompilerParams(
             vmem_limit_bytes=VMEM_BYTES, collective_id=0, has_side_effects=True

time: 61.4 us -> 58.5 us (0.953)
  Pallas kernels: 60.5 us -> 57.5 us
    pallas_call x1, Pallas kernels: 58 us -> 55 us  [small_group(): pl.pallas_call(functools.partial(fused_kernel, n_tok), in_specs=[main] *...]
where the time goes in v2:
time: 58.5 us; the launch traced here: 58.3 us
  Pallas kernels  57.5 us (98%)
  between operations  0.82 us (1%)
    pallas_call x1, Pallas kernels, small_group(): pl.pallas_call(functools.partial(fused_kernel, n_tok), in_specs=[main] *...  55 us
    pallas_call x1, Pallas kernels, small_group(): pl.pallas_call(store_kernel, in_specs=[pl.BlockSpec(memory_space=pl.ANY)]...  2.51 us

profile of v2, /device:TPU:0, one launch (start us, length us, event | category | flops | bytes accessed | tf_op | source)
XLA Modules:
  0.0 58.3 jit_solution(5473947640101638486)
XLA Ops:
  0.6 55.0 %fused.1 = (f32[4,192,768]{2,1,0:T(8,128)S(1)}, f32[768,768]{1,0:T(8,128)S(1)}, f32[256,768]{1,0:T(8,128)S(1)}) custom-call(bf16[384,768]{1,0:T(8,128)(2,1)} %bitcast.13, bf16[384,768]{1,0:T(8,128)(2,1)} %bitcast.14, bf16[768,3072]{1,0:T(8,128)(2,1)} %bitcast.8, bf16[3072,768]{1,0:T(8,128)(2,1)} %bitcast.9, f32[1,768]{1,0:T(1,128)} %gain1_in.1, ...), custom_call_target="tpu_custom_call" | custom-call | flops 21743271936 | bytes 18874368 | tf_op jit(solution)/shard_map/fused/pallas_call | solution.py:454
  55.6 2.5 %store.1 = (f32[192,3072]{1,0:T(8,128)}, f32[768,768]{1,0:T(8,128)}, f32[256,768]{1,0:T(8,128)}) custom-call(f32[4,192,768]{2,1,0:T(8,128)S(1)} %get-tuple-element.9.up_ref, f32[768,768]{1,0:T(8,128)S(1)} %get-tuple-element.10.down_ref, f32[256,768]{1,0:T(8,128)S(1)} %get-tuple-element.11.rows_ref), custom_call_target="tpu_custom_call" | custom-call | tf_op jit(solution)/shard_map/store/pallas_call | solution.py:502

commit v3 on v2

--- a/solution.py
+++ b/solution.py
@@ -134,9 +134,9 @@
     n_tok,
     mix_in, grad_in, up_in, down_in, gain1_in, gain2_in, owner_in, slot_in,
     gup_v, gdown_v, mine_v,
-    mix_v, mid_v, h_v, up_v, down_v, slope_v, act_v, hsel_v, wide_v, acc_v, grad_v,
+    mix_v, mid_v, h_v, up_v, down_v, slope_v, act_v, hsel_v, hlast_v, wide_v, acc_v, grad_v,
     sum_v, swap_v, embed_v, far_v, part_v, back_v, gain1_v, gain2_v, owner_v, slot_v,
-    up_sem, down_sem, load_sem, send_sem, recv_sem, swap_send, swap_recv, ready_sem, go_sem,
+    up_sem, down_sem, load_sem, send_sem, recv_sem, swap_send, swap_recv, ready_sem, go_sem, x_sem, y_sem,
 ):
     rows, width = grad_v.shape
     chunks, _, part = up_v.shape
@@ -149,7 +149,23 @@
     tok = lax.axis_index("token")
     col = lax.rem(me, 2)
     over_x = {"dp": me + 1 - 2 * col}
+    row = me // 2
     over_y = {"dp": lax.rem(me + 2, 4)}
+
+    barrier = pltpu.get_barrier_semaphore()
+
+    @pl.when(col == 0)
+    def _():
+        pl.semaphore_signal(barrier, inc=1, device_id=over_x, device_id_type=MESH)
+
+    @pl.when(row == 0)
+    def _():
+        pl.semaphore_signal(barrier, inc=1, device_id=over_y, device_id_type=MESH)
+
+    @pl.when(tok == 0)
+    def _():
+        for k in range(1, n_tok):
+            pl.semaphore_signal(barrier, inc=1, device_id={"token": k}, device_id_type=MESH)
 
     def group(g):
         return pl.ds(g * rows, rows)
@@ -184,38 +200,39 @@
     loads = [pltpu.make_async_copy(s, d, load_sem.at[i]) for i, (s, d) in enumerate(small)]
     loads[0].start()
     loads[1].start()
-    for j in range(chunks):
-        load_up(j).start()
-        load_down(j).start()
-    for load in loads[2:]:
-        load.start()
-
-    barrier = pltpu.get_barrier_semaphore()
-    for device in (over_x, over_y):
-        pl.semaphore_signal(barrier, inc=1, device_id=device, device_id_type=MESH)
-
-    @pl.when(tok == 0)
-    def _():
-        for k in range(1, n_tok):
-            pl.semaphore_signal(barrier, inc=1, device_id={"token": k}, device_id_type=MESH)
-        pl.semaphore_wait(barrier, 2)
+    load_up(0).start()
+    load_down(0).start()
+
+    needed = row + col + jnp.minimum(tok, 1)
+
+    @pl.when(needed > 0)
+    def _():
+        pl.semaphore_wait(barrier, needed)
 
     @pl.when(tok != 0)
     def _():
-        pl.semaphore_wait(barrier, 3)
         pl.semaphore_signal(ready_sem, inc=1, device_id={"token": 0}, device_id_type=MESH)
 
-    loads[0].wait()
-    mix_x = remote(0, mix_v.at[group(0)], mix_v.at[group(1)], over_x)
-    mix_y = remote(1, mix_v.at[group(0)], mix_v.at[group(2)], over_y)
+    mix_x = remote(0, mix_in, mix_v.at[group(1)], over_x)
+    mix_y = remote(1, mix_in, mix_v.at[group(2)], over_y)
     ids = [
         remote(2, owner_in, owner_v.at[1], over_x),
         remote(3, slot_in, slot_v.at[1], over_x),
         remote(4, owner_in, owner_v.at[2], over_y),
         remote(5, slot_in, slot_v.at[2], over_y),
     ]
-    for copy in [mix_x, mix_y] + ids:
-        copy.start()
+    @pl.when(col == 1)
+    def _():
+        pl.semaphore_signal(x_sem, inc=1, device_id=over_x, device_id_type=MESH)
+        mix_x.start()
+
+    @pl.when(row == 1)
+    def _():
+        pl.semaphore_signal(y_sem, inc=1, device_id=over_y, device_id_type=MESH)
+        mix_y.start()
+
+    def last_half(k):
+        return pl.ds(3 * rows + k * half_r, half_r)
 
     def norm_group(g):
         normed, _ = normalize(mix_v[group(g), :].astype(f32))
@@ -223,9 +240,13 @@
 
     def pick_group(g):
         shape = (hsel_v.shape[0], width)
-        row = lax.broadcasted_iota(jnp.int32, shape, 0) + me * shape[0]
-        pick = (row == lax.broadcasted_iota(jnp.int32, shape, 1)).astype(bf)
-        hsel_v[:, group(g)] = contract_cols(pick, h_v[group(g), :]).astype(bf)
+        line = lax.broadcasted_iota(jnp.int32, shape, 0) + me * shape[0]
+        pick = (line == lax.broadcasted_iota(jnp.int32, shape, 1)).astype(bf)
+        if g < 3:
+            hsel_v[:, group(g)] = contract_cols(pick, h_v[group(g), :]).astype(bf)
+        else:
+            for k in range(2):
+                hlast_v[k] = contract_cols(pick, h_v[last_half(k), :]).astype(bf)
 
     def activate(g, c):
         pres = [
@@ -243,14 +264,33 @@
                 total = more if total is None else total + more
         return total
 
+    loads[0].wait()
     loads[1].wait()
     norm_group(0)
     acc_v[...] = h_v[group(0), :].astype(f32)
 
-    @pl.loop(0, chunks, unroll=UNROLL)
-    def _(j):
+    @pl.when(col == 0)
+    def _():
+        pl.semaphore_wait(x_sem, 1)
+        mix_x.start()
+
+    @pl.when(row == 0)
+    def _():
+        pl.semaphore_wait(y_sem, 1)
+        mix_y.start()
+
+    for copy in ids:
+        copy.start()
+
+    for j in range(chunks):
         load_up(j).wait()
         load_down(j).wait()
+        if j + 1 < chunks:
+            load_up(j + 1).start()
+            load_down(j + 1).start()
+        else:
+            for load in loads[2:]:
+                load.start()
         acc_v[...] += activate(0, chunk_at(j))
 
     for load in loads[2:]:
@@ -270,11 +310,14 @@
         for k in range(1, n_tok):
             pl.semaphore_signal(go_sem, inc=1, device_id={"token": k}, device_id_type=MESH)
 
+    def slope_lines(lines, c):
+        grad_act = contract_cols(mid_v[lines, :], down_v[c])
+        grad_pre = (grad_act * slope_v[c, lines, :].astype(f32)).astype(bf)
+        slope_v[c, lines, :] = grad_pre
+        return grad_pre
+
     def slope_group(g, c):
-        grad_act = contract_cols(mid_v[group(g), :], down_v[c])
-        grad_pre = (grad_act * slope_v[c, group(g), :].astype(f32)).astype(bf)
-        slope_v[c, group(g), :] = grad_pre
-        return grad_pre
+        return slope_lines(group(g), c)
 
     acc_v[...] = wide_v[...]
 
@@ -336,8 +379,8 @@
     mid_y.wait_recv()
     mid_d = [
         remote(12, piece_of(1, 0), piece_of(3, 0), over_y),
-        remote(13, piece_of(2, 2), piece_of(3, 2), over_x),
-        remote(16, piece_of(1, 1), piece_of(3, 1), over_y),
+        remote(13, piece_of(2, 1), piece_of(3, 1), over_x),
+        remote(16, piece_of(1, 2), piece_of(3, 2), over_y),
         remote(17, piece_of(2, 3), piece_of(3, 3), over_x),
     ]
     mid_d[0].start()
@@ -374,6 +417,19 @@
     mix_dy.wait_recv()
     others(3)
 
+    def last_group(k):
+        lines = last_half(k)
+
+        @pl.loop(0, chunks, unroll=UNROLL)
+        def _(c):
+            gup_v[c] += contract_flat(hlast_v[k], slope_lines(lines, c))
+
+        gdown_v[...] += contract_rows(act_v[lines, :], mid_v[lines, :])
+
+    mid_d[0].wait_recv()
+    mid_d[1].wait_recv()
+    last_group(0)
+
     for copy in ids:
         copy.wait_recv()
     far_x.wait_recv()
@@ -381,8 +437,8 @@
 
     def hot(k, owner):
         target = owner_v[k] * hot_rows + slot_v[k]
-        row = lax.broadcasted_iota(jnp.int32, (hot_rows, rows), 0) + owner * hot_rows
-        return (row == target).astype(bf)
+        line = lax.broadcasted_iota(jnp.int32, (hot_rows, rows), 0) + owner * hot_rows
+        return (line == target).astype(bf)
 
     def merge(owner, k, cols):
         kept = contract_cols(hot(0, owner), embed_v[cols, :])
@@ -397,15 +453,9 @@
     mine_v[:, :half_w] = merge(me, 1, low)
     mine_v[:, half_w:] = merge(me, 2, high)
 
-    for copy in mid_d:
-        copy.wait_recv()
-
-    @pl.loop(0, chunks, unroll=UNROLL)
-    def _(c):
-        grad_pre = slope_group(3, c)
-        gup_v[c] += contract_flat(hsel_v[:, group(3)], grad_pre)
-
-    gdown_v[...] += contract_rows(act_v[group(3), :], mid_v[group(3), :])
+    mid_d[2].wait_recv()
+    mid_d[3].wait_recv()
+    last_group(1)
 
     back_y.wait_recv()
     back_x.wait_recv()
@@ -464,7 +514,8 @@
             vm((groups, part, width), bf),
             vm((groups, groups * rows, part), bf),
             vm((groups * rows, part), bf),
-            vm((own, groups * rows), bf),
+            vm((own, (groups - 1) * rows), bf),
+            vm((2, own, rows // 2), bf),
             vm((rows, width), f32),
             vm((rows, width), f32),
             vm((rows, width), bf),
@@ -487,6 +538,8 @@
             dma((n_tok - 1,)),
             pltpu.SemaphoreType.REGULAR,
             pltpu.SemaphoreType.REGULAR,
+            pltpu.SemaphoreType.REGULAR,
+            pltpu.SemaphoreType.REGULAR,
         ],
         compiler_params=pltpu.CompilerParams(
             vmem_limit_bytes=VMEM_BYTES, collective_id=0, has_side_effects=True

time: 58.5 us -> 57.4 us (0.981)
  Pallas kernels: 57.5 us -> 56.4 us
    pallas_call x1, Pallas kernels: 55 us -> 53.9 us  [small_group(): pl.pallas_call(functools.partial(fused_kernel, n_tok), in_specs=[main] *...]
where the time goes in v3:
time: 57.4 us; the launch traced here: 57.2 us
  Pallas kernels  56.4 us (98%)
  between operations  0.82 us (1%)
    pallas_call x1, Pallas kernels, small_group(): pl.pallas_call(functools.partial(fused_kernel, n_tok), in_specs=[main] *...  53.9 us
    pallas_call x1, Pallas kernels, small_group(): pl.pallas_call(store_kernel, in_specs=[pl.BlockSpec(memory_space=pl.ANY)]...  2.51 us

profile of v3, /device:TPU:0, one launch (start us, length us, event | category | flops | bytes accessed | tf_op | source)
XLA Modules:
  0.0 57.2 jit_solution(12428243528434500608)
XLA Ops:
  0.6 53.9 %fused.1 = (f32[4,192,768]{2,1,0:T(8,128)S(1)}, f32[768,768]{1,0:T(8,128)S(1)}, f32[256,768]{1,0:T(8,128)S(1)}) custom-call(bf16[384,768]{1,0:T(8,128)(2,1)} %bitcast.13, bf16[384,768]{1,0:T(8,128)(2,1)} %bitcast.14, bf16[768,3072]{1,0:T(8,128)(2,1)} %bitcast.8, bf16[3072,768]{1,0:T(8,128)(2,1)} %bitcast.9, f32[1,768]{1,0:T(1,128)} %gain1_in.1, ...), custom_call_target="tpu_custom_call" | custom-call | flops 21743271936 | bytes 18874368 | tf_op jit(solution)/shard_map/fused/pallas_call | solution.py:504
  54.5 2.5 %store.1 = (f32[192,3072]{1,0:T(8,128)}, f32[768,768]{1,0:T(8,128)}, f32[256,768]{1,0:T(8,128)}) custom-call(f32[4,192,768]{2,1,0:T(8,128)S(1)} %get-tuple-element.9.up_ref, f32[768,768]{1,0:T(8,128)S(1)} %get-tuple-element.10.down_ref, f32[256,768]{1,0:T(8,128)S(1)} %get-tuple-element.11.rows_ref), custom_call_target="tpu_custom_call" | custom-call | tf_op jit(solution)/shard_map/store/pallas_call | solution.py:555

commit v4 on v3

--- a/solution.py
+++ b/solution.py
@@ -401,8 +401,6 @@
     far_y = remote(11, embed_v.at[high], far_v.at[1], over_y)
     far_x.start()
     far_y.start()
-    mid_d[2].start()
-    mid_d[3].start()
 
     gdown_v[...] = contract_rows(act_v[pair, :], mid_v[pair, :])
 
@@ -413,6 +411,8 @@
 
     gdown_v[...] += contract_rows(act_v[group(2), :], mid_v[group(2), :])
 
+    mid_d[2].start()
+    mid_d[3].start()
     mix_dx.wait_recv()
     mix_dy.wait_recv()
     others(3)
@@ -457,13 +457,13 @@
     mid_d[3].wait_recv()
     last_group(1)
 
-    back_y.wait_recv()
-    back_x.wait_recv()
-    mine_v[:, :half_w] += back_v[0].astype(f32)
-    mine_v[:, half_w:] += back_v[1].astype(f32)
-
     for copy in [mix_x, mix_y] + ids + [mid_x, mid_y, mix_dx, mix_dy] + swaps:
         copy.wait_send()
+    back_y.wait_recv()
+    mine_v[:, :half_w] += back_v[0].astype(f32)
+    back_x.wait_recv()
+    mine_v[:, half_w:] += back_v[1].astype(f32)
+
     for copy in [far_x, far_y, back_x, back_y] + mid_d:
         copy.wait_send()
 

time: 57.4 us -> 57.4 us (level)
  no operation moved by 1% of the time
where the time goes in v4:
time: 57.4 us; the launch traced here: 57.2 us
  Pallas kernels  56.3 us (98%)
  between operations  0.82 us (1%)
    pallas_call x1, Pallas kernels, small_group(): pl.pallas_call(functools.partial(fused_kernel, n_tok), in_specs=[main] *...  53.8 us
    pallas_call x1, Pallas kernels, small_group(): pl.pallas_call(store_kernel, in_specs=[pl.BlockSpec(memory_space=pl.ANY)]...  2.51 us

profile of v4, /device:TPU:0, one launch (start us, length us, event | category | flops | bytes accessed | tf_op | source)
XLA Modules:
  0.0 57.2 jit_solution(12288195591944840211)
XLA Ops:
  0.6 53.8 %fused.1 = (f32[4,192,768]{2,1,0:T(8,128)S(1)}, f32[768,768]{1,0:T(8,128)S(1)}, f32[256,768]{1,0:T(8,128)S(1)}) custom-call(bf16[384,768]{1,0:T(8,128)(2,1)} %bitcast.13, bf16[384,768]{1,0:T(8,128)(2,1)} %bitcast.14, bf16[768,3072]{1,0:T(8,128)(2,1)} %bitcast.8, bf16[3072,768]{1,0:T(8,128)(2,1)} %bitcast.9, f32[1,768]{1,0:T(1,128)} %gain1_in.1, ...), custom_call_target="tpu_custom_call" | custom-call | flops 21743271936 | bytes 18874368 | tf_op jit(solution)/shard_map/fused/pallas_call | solution.py:504
  54.5 2.5 %store.1 = (f32[192,3072]{1,0:T(8,128)}, f32[768,768]{1,0:T(8,128)}, f32[256,768]{1,0:T(8,128)}) custom-call(f32[4,192,768]{2,1,0:T(8,128)S(1)} %get-tuple-element.9.up_ref, f32[768,768]{1,0:T(8,128)S(1)} %get-tuple-element.10.down_ref, f32[256,768]{1,0:T(8,128)S(1)} %get-tuple-element.11.rows_ref), custom_call_target="tpu_custom_call" | custom-call | tf_op jit(solution)/shard_map/store/pallas_call | solution.py:555
